TPU v7x, 256 devices: a whole 4x4x8 slice. The times are simulated.
256 devices in a mesh: row: 8 (over x, core), col: 32 (over y, z).
Axes of the slice: x: 4, y: 4, z: 8, core: 2. Of those that a mesh axis runs over, the one named last changes fastest.
Arguments:
- affinity_tiles: bfloat16 [1024, 64, 128, 128], P(('row', 'col'))
- block_columns: int32 [1024, 64], P(('row', 'col')), may hold values from 0 to 127, as said below
- live_counts: int32 [8, 128], P('row', 'col'), may hold values from 1 to 64, 4096 in all within a row
- earlier_blocks: float32 [4, 64, 131072], P(None, None, ('row', 'col')), may hold values from -6 to 6
Outputs:
- new_blocks: float32 [2, 64, 131072], P(None, None, ('row', 'col'))
- triangular_factors: float32 [2, 64, 64], replicated
Inputs may be any that keep to these rules, and one draw needn't show every extreme that they name: `block_columns`: slot 0 of every block row names the block row itself; columns name block rows of the same row group. `live_counts`: slots at or past a block row's count are ignored.
All inputs are finite; a program needn't handle non-finite values.
Results may differ from a plain program's by a relative error of at most 0.0059.
Values may be sent and summed in bfloat16 or wider, within the bound.
No kernel may reach another device: no remote copies, remote signals or barrier semaphores. Data moves between devices by JAX's collectives and lax.ppermute only.
A program may use at most 64 MiB of HBM per device.

v0:
```python
import jax
import jax.numpy as jnp
from jax import lax
from jax.sharding import PartitionSpec as P

STEPS = 2


def apply_tiles(affinity_tiles, block_columns, row_counts, group_blocks):
    block_rows = affinity_tiles.shape[0]
    slot_count = affinity_tiles.shape[1]
    tile_size = affinity_tiles.shape[2]
    block_width = group_blocks.shape[0]
    slot_ids = lax.broadcasted_iota(jnp.int32, (block_rows, slot_count), 1)
    live_mask = slot_ids < row_counts[:, None]
    picked = jnp.take(group_blocks, block_columns, axis=1)
    picked = jnp.where(live_mask[None, :, :, None], picked, jnp.zeros((), jnp.bfloat16))
    running = jnp.einsum(
        "rsij,brsj->bri", affinity_tiles, picked, preferred_element_type=jnp.float32
    )
    return running.reshape(block_width, block_rows * tile_size)


def on_device(affinity_tiles, block_columns, live_counts, earlier_blocks):
    block_rows = affinity_tiles.shape[0]
    tile_size = affinity_tiles.shape[2]
    block_width = earlier_blocks.shape[1]
    rows_here = earlier_blocks.shape[2]
    total_rows = rows_here * lax.axis_size("row") * lax.axis_size("col")
    row_counts = live_counts.reshape(block_rows)
    known_list = [earlier_blocks[i] for i in range(earlier_blocks.shape[0])]
    first_half = known_list[-1].astype(jnp.bfloat16)
    group_half = lax.all_gather(first_half, "col", axis=1, tiled=True)
    fresh_list = []
    factor_list = []
    for step_index in range(STEPS):
        is_last = step_index + 1 == STEPS
        group_blocks = group_half.reshape(block_width, -1, tile_size)
        product = apply_tiles(affinity_tiles, block_columns, row_counts, group_blocks)
        known = jnp.concatenate(known_list, 0)
        local_proj = jnp.dot(known, product.T, precision=lax.Precision.HIGHEST) / total_rows
        projections = lax.psum(local_proj, ("row", "col"))
        residual = product - jnp.dot(projections.T, known, precision=lax.Precision.HIGHEST)
        local_gram = jnp.dot(residual, residual.T, precision=lax.Precision.HIGHEST) / total_rows
        gram_sum = lax.psum(local_gram, ("row", "col"))
        factor_low = jnp.linalg.cholesky(gram_sum)
        fresh = jax.scipy.linalg.solve_triangular(factor_low, residual, lower=True)
        fresh_list.append(fresh)
        factor_list.append(factor_low.T)
        known_list.append(fresh)
        if not is_last:
            group_half = lax.all_gather(fresh.astype(jnp.bfloat16), "col", axis=1, tiled=True)
    return (jnp.stack(fresh_list), jnp.stack(factor_list))


def solution(mesh):
    return jax.shard_map(
        on_device,
        mesh=mesh,
        in_specs=(
            P(("row", "col"), None, None, None),
            P(("row", "col"), None),
            P("row", "col"),
            P(None, None, ("row", "col")),
        ),
        out_specs=(P(None, None, ("row", "col")), P()),
        check_vma=False,
    )
```

profile of v0, /device:TPU:1, one launch (start us, length us, event | category | flops | bytes accessed | tf_op | source)
XLA Modules:
  0.0 864.7 jit_solution(17645085274301516106)
XLA Ops:
  7.2 1.5 fusion.32
  11.3 0.9 constant_dynamic-update-slice_fusion.3
  13.1 1.1 slice_bitcast_fusion.2
  14.3 71.6 %all-gather.3.cloned.1.call-done = bf16[64,16384]{1,0:T(8,128)(2,1)} async-done(((bf16[64,512]{1,0:T(8,128)(2,1)}), bf16[64,16384]{1,0:T(8,128)(2,1)}) %all-gather.3.cloned.1.call-update) | async-done | bytes 2097168 | tf_op jit(solution)/shard_map/all_gather | solution.py:33
  85.9 2.2 copy_bitcast_fusion.1
  88.1 3.0 gather_fusion
  91.1 6.3 fusion.12
  97.3 1.2 convolution_multiply_fusion.1
  99.6 246.5 %all-reduce.3.cloned.1.call-done = f32[256,64]{1,0:T(8,128)} async-done(((f32[256,64]{1,0:T(8,128)}), f32[256,64]{1,0:T(8,128)}) %all-reduce.3.cloned.1.call-update) | async-done | bytes 65552 | tf_op jit(solution)/shard_map/psum | solution.py:42
  346.0 1.3 convolution_subtract_fusion.1
  347.6 76.2 %psum.29 = f32[64,64]{0,1:T(8,128)S(1)} all-reduce(f32[64,64]{0,1:T(8,128)S(1)} %convolution_multiply_fusion.3), channel_id=1, replica_groups=mesh['row'=8,'col'=32] {'row','col'}, use_global_device_ids=true, to_apply=%region_1.3 | all-reduce | flops 4096 | bytes 32768 | tf_op jit(solution)/shard_map/psum | solution.py:45
  423.9 5.8 cholesky.44
  431.1 4.9 custom-call.6
  436.0 1.0 fusion.33
  437.0 66.8 %all-gather.5.cloned.1.call-done = bf16[64,16384]{1,0:T(8,128)(2,1)} async-done(((bf16[64,512]{1,0:T(8,128)(2,1)}), bf16[64,16384]{1,0:T(8,128)(2,1)}) %all-gather.5.cloned.1.call-update) | async-done | bytes 2097168 | tf_op jit(solution)/shard_map/all_gather | solution.py:52
  503.8 2.2 copy_bitcast_fusion
  506.0 3.0 gather_fusion.1
  509.0 6.3 fusion.13
  515.3 1.3 convolution_multiply_fusion
  516.7 251.0 %all-reduce.5.cloned.1.call-done = f32[320,64]{1,0:T(8,128)} async-done(((f32[320,64]{1,0:T(8,128)}), f32[320,64]{1,0:T(8,128)}) %all-reduce.5.cloned.1.call-update) | async-done | bytes 81936 | tf_op jit(solution)/shard_map/psum | solution.py:42
  767.7 1.5 convolution_subtract_fusion
  769.4 74.8 %psum.31 = f32[64,64]{0,1:T(8,128)S(1)} all-reduce(f32[64,64]{0,1:T(8,128)S(1)} %convolution_multiply_fusion.2), channel_id=1, replica_groups=mesh['row'=8,'col'=32] {'row','col'}, use_global_device_ids=true, to_apply=%region_5.9 | all-reduce | flops 4096 | bytes 32768 | tf_op jit(solution)/shard_map/psum | solution.py:45
  844.3 5.8 cholesky.55
  852.2 4.9 custom-call.7
  (31 shorter events, 9.6 us)
Async XLA Ops:
  7.2 78.7 %all-gather.3.cloned.1.call-start = ((), (), s32[]{:S(2)}) async-start(), calls=%async_computation | async-start | bytes 2162688 | tf_op jit(solution)/shard_map/all_gather | solution.py:33
  8.8 337.2 %all-reduce.3.cloned.1.call-start = ((), (), s32[]{:S(2)}) async-start(), calls=%async_computation.1 | async-start | bytes 262144 | tf_op jit(solution)/shard_map/psum | solution.py:42
  98.6 405.2 %all-gather.5.cloned.1.call-start = ((), (), s32[]{:S(2)}) async-start(), calls=%async_computation.2 | async-start | bytes 2162688 | tf_op jit(solution)/shard_map/all_gather | solution.py:52
  437.0 330.7 %all-reduce.5.cloned.1.call-start = ((), (), s32[]{:S(2)}) async-start(), calls=%async_computation.3 | async-start | bytes 327680 | tf_op jit(solution)/shard_map/psum | solution.py:42
Sparse Core Ops, SparseCore 0:
  11.0 74.8 all-gather.2
  98.7 247.2 all-reduce.2
  437.1 66.6 all-gather.4
  516.8 250.8 all-reduce.4
where the time goes:
time: 865 us
  waiting for transfers between devices  636 us (74%)
  blocking collectives  151 us (17%)
  other arithmetic  26.4 us (3%)
  matrix products  19.7 us (2%)
  local copies, waits for them, and re-layouts  17.7 us (2%)
  between operations  13.9 us (2%)
    psum x2, waiting for transfers between devices, on_device(): projections = lax.psum(local_proj, ('row', 'col'))  497 us
    psum x2, blocking collectives, on_device(): gram_sum = lax.psum(local_gram, ('row', 'col'))  151 us
    all_gather x1, waiting for transfers between devices, on_device(): group_half = lax.all_gather(first_half, 'col', axis=1, tiled=True)  71.6 us
    all_gather x1, waiting for transfers between devices, on_device(): lax.all_gather(fresh.astype(jnp.bfloat16), 'col', axis=1, tiled=True)  66.8 us
  transfers between devices with their start and end apart: 4, of which 4 were waited for; matrix products, arithmetic and copies ran while one was open for 1% of the time, Pallas kernels for 0%

commit v1 on v0

--- a/solution.py
+++ b/solution.py
@@ -39,7 +39,15 @@
         product = apply_tiles(affinity_tiles, block_columns, row_counts, group_blocks)
         known = jnp.concatenate(known_list, 0)
         local_proj = jnp.dot(known, product.T, precision=lax.Precision.HIGHEST) / total_rows
-        projections = lax.psum(local_proj, ("row", "col"))
+
+        def form_wires(patch):
+            axis_name = "row"
+            mesh_dim = "col"
+            for num in (axis_name, mesh_dim):
+                patch = jax.lax.psum(patch, num)
+            return patch
+
+        projections = form_wires(local_proj)
         residual = product - jnp.dot(projections.T, known, precision=lax.Precision.HIGHEST)
         local_gram = jnp.dot(residual, residual.T, precision=lax.Precision.HIGHEST) / total_rows
         gram_sum = lax.psum(local_gram, ("row", "col"))

time: 865 us -> 791 us (0.914)
  waiting for transfers between devices: 636 us -> 557 us
    psum x2 -> x4, waiting for transfers between devices: 497 us -> 417 us  [form_wires(): patch = jax.lax.psum(patch, num)]
  transfers between devices with their start and end apart: 4 -> 6, of which waited for: 4 -> 6; matrix products, arithmetic and copies ran while one was open for 1% -> 1% of each run, Pallas kernels for 0% -> 0%
where the time goes in v1:
time: 791 us
  waiting for transfers between devices  557 us (70%)
  blocking collectives  157 us (20%)
  other arithmetic  26.4 us (3%)
  matrix products  19.7 us (2%)
  local copies, waits for them, and re-layouts  15.9 us (2%)
  between operations  14.3 us (2%)
    psum x4, waiting for transfers between devices, form_wires(): patch = jax.lax.psum(patch, num)  417 us
    psum x2, blocking collectives, on_device(): gram_sum = lax.psum(local_gram, ('row', 'col'))  157 us
    all_gather x1, waiting for transfers between devices, on_device(): group_half = lax.all_gather(first_half, 'col', axis=1, tiled=True)  72.5 us
    all_gather x1, waiting for transfers between devices, on_device(): lax.all_gather(fresh.astype(jnp.bfloat16), 'col', axis=1, tiled=True)  67.5 us
  transfers between devices with their start and end apart: 6, of which 6 were waited for; matrix products, arithmetic and copies ran while one was open for 1% of the time, Pallas kernels for 0%

profile of v1, /device:TPU:1, one launch (start us, length us, event | category | flops | bytes accessed | tf_op | source)
XLA Modules:
  0.0 791.0 jit_solution(10278536077870864292)
XLA Ops:
  7.2 1.5 fusion.32
  12.2 1.1 slice_bitcast_fusion.2
  13.4 72.5 %all-gather.3.cloned.1.call-done = bf16[64,16384]{1,0:T(8,128)(2,1)} async-done(((bf16[64,512]{1,0:T(8,128)(2,1)}), bf16[64,16384]{1,0:T(8,128)(2,1)}) %all-gather.3.cloned.1.call-update) | async-done | bytes 2097168 | tf_op jit(solution)/shard_map/all_gather | solution.py:33
  85.9 2.2 copy_bitcast_fusion.1
  88.1 3.0 gather_fusion
  91.1 6.3 fusion.12
  97.4 1.2 convolution_multiply_fusion.1
  98.7 65.6 %all-reduce.5.cloned.1.call-done = f32[256,64]{1,0:T(8,128)} async-done(((f32[256,64]{1,0:T(8,128)}), f32[256,64]{1,0:T(8,128)}) %all-reduce.5.cloned.1.call-update) | async-done | bytes 65552 | tf_op jit(solution)/shard_map/psum | solution.py:47
  164.4 142.8 %all-reduce.7.cloned.1.call-done = f32[256,64]{1,0:T(8,128)} async-done(((f32[256,64]{1,0:T(8,128)}), f32[256,64]{1,0:T(8,128)}) %all-reduce.7.cloned.1.call-update) | async-done | bytes 65552 | tf_op jit(solution)/shard_map/psum | solution.py:47
  307.2 1.3 convolution_subtract_fusion.1
  308.7 78.2 %psum.44 = f32[64,64]{0,1:T(8,128)S(1)} all-reduce(f32[64,64]{0,1:T(8,128)S(1)} %convolution_multiply_fusion.3), channel_id=1, replica_groups=mesh['row'=8,'col'=32] {'row','col'}, use_global_device_ids=true, to_apply=%region_2.4 | all-reduce | flops 4096 | bytes 32768 | tf_op jit(solution)/shard_map/psum | solution.py:53
  387.0 5.8 cholesky.44
  394.2 4.9 custom-call.6
  400.1 67.5 %all-gather.5.cloned.1.call-done = bf16[64,16384]{1,0:T(8,128)(2,1)} async-done(((bf16[64,512]{1,0:T(8,128)(2,1)}), bf16[64,16384]{1,0:T(8,128)(2,1)}) %all-gather.5.cloned.1.call-update) | async-done | bytes 2097168 | tf_op jit(solution)/shard_map/all_gather | solution.py:60
  467.6 2.2 copy_bitcast_fusion
  469.8 3.0 gather_fusion.1
  472.8 6.3 fusion.13
  479.1 1.3 convolution_multiply_fusion
  480.5 65.9 %all-reduce.9.cloned.1.call-done = f32[320,64]{1,0:T(8,128)} async-done(((f32[320,64]{1,0:T(8,128)}), f32[320,64]{1,0:T(8,128)}) %all-reduce.9.cloned.1.call-update) | async-done | bytes 81936 | tf_op jit(solution)/shard_map/psum | solution.py:47
  546.5 142.8 %all-reduce.11.cloned.1.call-done = f32[320,64]{1,0:T(8,128)} async-done(((f32[320,64]{1,0:T(8,128)}), f32[320,64]{1,0:T(8,128)}) %all-reduce.11.cloned.1.call-update) | async-done | bytes 81936 | tf_op jit(solution)/shard_map/psum | solution.py:47
  689.3 1.5 convolution_subtract_fusion
  691.1 79.1 %psum.47 = f32[64,64]{0,1:T(8,128)S(1)} all-reduce(f32[64,64]{0,1:T(8,128)S(1)} %convolution_multiply_fusion.2), channel_id=1, replica_groups=mesh['row'=8,'col'=32] {'row','col'}, use_global_device_ids=true, to_apply=%region_7.11 | all-reduce | flops 4096 | bytes 32768 | tf_op jit(solution)/shard_map/psum | solution.py:53
  770.2 5.8 cholesky.55
  778.1 4.9 custom-call.7
  (39 shorter events, 9.8 us)
Async XLA Ops:
  7.2 78.7 %all-gather.3.cloned.1.call-start = ((), (), s32[]{:S(2)}) async-start(), calls=%async_computation | async-start | bytes 2162688 | tf_op jit(solution)/shard_map/all_gather | solution.py:33
  8.8 155.5 %all-reduce.5.cloned.1.call-start = ((), (), s32[]{:S(2)}) async-start(), calls=%async_computation.1 | async-start | bytes 262144 | tf_op jit(solution)/shard_map/psum | solution.py:47
  91.1 7.6 copy-start
  98.6 208.5 %all-reduce.7.cloned.1.call-start = ((), (), s32[]{:S(2)}) async-start(), calls=%async_computation.2 | async-start | bytes 262144 | tf_op jit(solution)/shard_map/psum | solution.py:47
  164.3 303.3 %all-gather.5.cloned.1.call-start = ((), (), s32[]{:S(2)}) async-start(), calls=%async_computation.3 | async-start | bytes 2162688 | tf_op jit(solution)/shard_map/all_gather | solution.py:60
  400.1 146.4 %all-reduce.9.cloned.1.call-start = ((), (), s32[]{:S(2)}) async-start(), calls=%async_computation.4 | async-start | bytes 327680 | tf_op jit(solution)/shard_map/psum | solution.py:47
  480.5 208.9 %all-reduce.11.cloned.1.call-start = ((), (), s32[]{:S(2)}) async-start(), calls=%async_computation.5 | async-start | bytes 327680 | tf_op jit(solution)/shard_map/psum | solution.py:47
Sparse Core Ops, SparseCore 0:
  11.0 74.8 all-gather.2
  98.8 65.4 all-reduce.4
  167.8 139.3 all-reduce.6
  400.2 67.3 all-gather.4
  480.6 65.8 all-reduce.8
  549.8 139.5 all-reduce.10
